TPU v7x, 32 devices: a whole 2x2x4 slice. The times are simulated.
32 devices in a mesh: ctx: 8 (over y, x, core), wa: 4 (over z).
Axes of the slice: x: 2, y: 2, z: 4, core: 2. Of those that a mesh axis runs over, the one named last changes fastest.
Arguments:
- tokens: bfloat16 [4, 1024, 2048], P('wa', 'ctx'), may hold values from -6 to 6
- lengths: int32 [4, 2], P('wa'), may hold values from 384 to 640, as said below
- dealing: int32 [4, 8], P('wa'), may hold values from 0 to 7, each once within a row
- norm1_gain: float32 [2048], replicated, may hold values from 0.1 to 1.9
- w_qkv: bfloat16 [2048, 6144], P('wa'), may hold values from -0.125 to 0.125
- w_out: bfloat16 [2048, 2048], P('wa'), may hold values from -2 to 2
- norm2_gain: float32 [2048], replicated, may hold values from 0.1 to 1.9
- w_gate_up: bfloat16 [2048, 11008], P('wa'), may hold values from -0.125 to 0.125
- w_down: bfloat16 [5504, 2048], P('wa'), may hold values from -0.078125 to 0.078125
- grad_out: bfloat16 [4, 1024, 2048], P('wa', 'ctx'), may hold values from -6 to 6
Outputs:
- out: bfloat16 [4, 1024, 2048], P('wa', 'ctx')
- d_tokens: bfloat16 [4, 1024, 2048], P('wa', 'ctx')
- d_norm1_gain: float32 [2048], replicated
- d_w_qkv: float32 [2048, 6144], P('wa')
- d_w_out: float32 [2048, 2048], P('wa')
- d_norm2_gain: float32 [2048], replicated
- d_w_gate_up: float32 [2048, 11008], P('wa')
- d_w_down: float32 [5504, 2048], P('wa')
Inputs may be any that keep to these rules, and one draw needn't show every extreme that they name: Each row holds the lengths of the two sequences of that group, first sequence first; they sum to 1024; some row holds a sequence of exactly 384 tokens. `dealing`: each row is a permutation of the block numbers of the group.
All inputs are finite; a program needn't handle non-finite values.
Results may differ from a plain program's by a relative error of at most 0.019.
Values may be sent and summed in bfloat16 or wider, within the bound.
A program may use at most 576 MiB of HBM per device.

v0:
```python
import math
import jax
import jax.numpy as jnp
from jax import lax
from jax.sharding import PartitionSpec as P

HEADS = 16
HEAD = 128
FF = 5504
WINDOW = 2048
BLOCK = 128
EPSILON = 1e-06


def dot_plain(left, right):
    return jnp.dot(left, right, preferred_element_type=jnp.float32)


def dot_right_t(left, right):
    return lax.dot_general(
        left, right, (((1,), (1,)), ((), ())), preferred_element_type=jnp.float32
    )


def dot_left_t(left, right):
    return lax.dot_general(
        left, right, (((0,), (0,)), ((), ())), preferred_element_type=jnp.float32
    )


def rms_scale(values):
    return lax.rsqrt(jnp.mean(values * values, axis=-1, keepdims=True) + EPSILON)


def rotary_tables(seq_pos):
    half_width = HEAD // 2
    inverse_freq = jnp.power(10000.0, -2.0 * jnp.arange(half_width, dtype=jnp.float32) / HEAD)
    angles = seq_pos.astype(jnp.float32)[:, None] * inverse_freq[None, :]
    return (jnp.cos(angles)[:, None, :], jnp.sin(angles)[:, None, :])


def rotate(values, cosine, sine):
    half_width = HEAD // 2
    first_half = values[..., :half_width]
    second_half = values[..., half_width:]
    return jnp.concatenate(
        [first_half * cosine - second_half * sine, first_half * sine + second_half * cosine],
        axis=-1,
    )


def unrotate(values, cosine, sine):
    half_width = HEAD // 2
    first_half = values[..., :half_width]
    second_half = values[..., half_width:]
    return jnp.concatenate(
        [first_half * cosine + second_half * sine, second_half * cosine - first_half * sine],
        axis=-1,
    )


def row_picker(targets, carried, segment):
    inside = (targets >= 0) & (targets < segment.shape[0])
    taken_rows = jnp.take(segment, jnp.clip(targets, 0, segment.shape[0] - 1), axis=0)
    return jnp.where(inside[:, None], taken_rows, carried)


def per_device(
    tokens, lengths, dealing, norm1_gain, w_qkv, w_out, norm2_gain, w_gate_up, w_down, grad_out
):
    tok_rows = tokens.shape[1]
    width = tokens.shape[2]
    ctx_index = lax.axis_index("ctx")
    block_order = dealing[0]
    block_total = block_order.shape[0]
    group_rows = block_total * BLOCK
    own_blocks = tok_rows // BLOCK
    first_length = lengths[0, 0]
    in_block = jnp.arange(BLOCK, dtype=jnp.int32)
    key_pos = jnp.repeat(block_order, BLOCK) * BLOCK + jnp.tile(in_block, block_total)
    key_seg = (key_pos >= first_length).astype(jnp.int32)
    query_pos = lax.dynamic_slice_in_dim(key_pos, ctx_index * tok_rows, tok_rows)
    query_seg = lax.dynamic_slice_in_dim(key_seg, ctx_index * tok_rows, tok_rows)
    cosine, sine = rotary_tables(query_pos - query_seg * first_length)
    distance = query_pos[:, None] - key_pos[None, :]
    allowed = (query_seg[:, None] == key_seg[None, :]) & (distance >= 0) & (distance < WINDOW)
    block_ids = jnp.arange(block_total, dtype=jnp.int32)
    inverse = jnp.sum(
        jnp.where(block_order[None, :] == block_ids[:, None], block_ids[None, :], 0), axis=1
    )
    own_sources = lax.dynamic_slice_in_dim(inverse, ctx_index * own_blocks, own_blocks)
    source_rows = jnp.repeat(own_sources, BLOCK) * BLOCK + jnp.tile(in_block, own_blocks)
    empty_rows = jnp.zeros((tok_rows, width), jnp.bfloat16)
    cotangent = row_picker(
        query_pos, empty_rows, lax.all_gather(grad_out[0], "ctx", axis=0, tiled=True)
    )
    inputs = tokens[0].astype(jnp.float32)
    scale_one = rms_scale(inputs)
    normed_one = inputs * scale_one
    act_one = (normed_one * norm1_gain).astype(jnp.bfloat16)
    full_qkv, full_out = (
        lax.all_gather(w_qkv, "wa", axis=0, tiled=True),
        lax.all_gather(w_out, "wa", axis=0, tiled=True),
    )
    projected = dot_plain(act_one, full_qkv)
    query_b = rotate(projected[:, :width].reshape(tok_rows, HEADS, HEAD), cosine, sine).astype(
        jnp.bfloat16
    )
    key_b = rotate(
        projected[:, width : 2 * width].reshape(tok_rows, HEADS, HEAD), cosine, sine
    ).astype(jnp.bfloat16)
    value_b = projected[:, 2 * width :].astype(jnp.bfloat16)
    kv_local = jnp.concatenate([key_b.reshape(tok_rows, width), value_b], axis=1)
    kv_all = lax.all_gather(kv_local, "ctx", axis=0, tiled=True)
    keys_all = kv_all[:, :width].reshape(group_rows, HEADS, HEAD)
    values_all = kv_all[:, width:].reshape(group_rows, HEADS, HEAD)
    score_scale = math.sqrt(HEAD)
    per_group = min(4, HEADS)
    mixed_parts = []
    total_parts = []
    for head_first in range(0, HEADS, per_group):
        query_part = query_b[:, head_first : head_first + per_group]
        key_part = keys_all[:, head_first : head_first + per_group]
        value_part = values_all[:, head_first : head_first + per_group]
        scores = (
            jnp.einsum("qhe,khe->hqk", query_part, key_part, preferred_element_type=jnp.float32)
            / score_scale
        )
        scores = jnp.where(allowed[None], scores, -jnp.inf)
        largest = jnp.max(scores, axis=2, keepdims=True)
        log_total = largest + jnp.log(jnp.sum(jnp.exp(scores - largest), axis=2, keepdims=True))
        probs_b = jnp.exp(scores - log_total).astype(jnp.bfloat16)
        mixed_parts.append(
            jnp.einsum("hqk,khe->qhe", probs_b, value_part, preferred_element_type=jnp.float32)
        )
        total_parts.append(log_total[:, :, 0])
    log_totals = jnp.concatenate(total_parts, axis=0)
    attended_b = jnp.concatenate(mixed_parts, axis=1).reshape(tok_rows, width).astype(jnp.bfloat16)
    hidden = inputs + dot_plain(attended_b, full_out)
    scale_two = rms_scale(hidden)
    normed_two = hidden * scale_two
    act_two = (normed_two * norm2_gain).astype(jnp.bfloat16)
    full_gate_up, full_down = (
        lax.all_gather(w_gate_up, "wa", axis=0, tiled=True),
        lax.all_gather(w_down, "wa", axis=0, tiled=True),
    )
    gate_up = dot_plain(act_two, full_gate_up)
    gate_part = gate_up[:, :FF]
    up_part = gate_up[:, FF:]
    sigmoid_gate = jax.nn.sigmoid(gate_part)
    silu_gate = gate_part * sigmoid_gate
    inner_b = (silu_gate * up_part).astype(jnp.bfloat16)
    result_b = (hidden + dot_plain(inner_b, full_down)).astype(jnp.bfloat16)
    out_given = row_picker(
        source_rows, empty_rows, lax.all_gather(result_b, "ctx", axis=0, tiled=True)
    )
    back_gate_up, back_down = (
        lax.all_gather(w_gate_up, "wa", axis=0, tiled=True),
        lax.all_gather(w_down, "wa", axis=0, tiled=True),
    )
    down_share = lax.psum_scatter(
        dot_left_t(inner_b, cotangent).astype(jnp.bfloat16), "wa", scatter_dimension=0, tiled=True
    )
    d_inner = dot_right_t(cotangent, back_down)
    d_gate = d_inner * up_part * sigmoid_gate * (1.0 + gate_part * (1.0 - sigmoid_gate))
    d_gate_up_b = jnp.concatenate([d_gate, d_inner * silu_gate], axis=1).astype(jnp.bfloat16)
    gate_up_share = lax.psum_scatter(
        dot_left_t(act_two, d_gate_up_b).astype(jnp.bfloat16), "wa", scatter_dimension=0, tiled=True
    )
    d_normed_two = dot_right_t(d_gate_up_b, back_gate_up)
    gain_two_part = jnp.sum(d_normed_two * normed_two, axis=0)
    scaled_two = d_normed_two * norm2_gain
    d_hidden = cotangent.astype(jnp.float32) + scale_two * (
        scaled_two - normed_two * jnp.mean(scaled_two * normed_two, axis=1, keepdims=True)
    )
    d_branch_b = d_hidden.astype(jnp.bfloat16)
    back_qkv, back_out = (
        lax.all_gather(w_qkv, "wa", axis=0, tiled=True),
        lax.all_gather(w_out, "wa", axis=0, tiled=True),
    )
    grad_mixed_b = (
        dot_right_t(d_branch_b, back_out).astype(jnp.bfloat16).reshape(tok_rows, HEADS, HEAD)
    )
    head_steps = HEADS // per_group

    def make_backward():

        def backward_heads(head_index, carried):
            d_query, d_keys_values, row_dots = carried
            head_first = head_index * per_group
            query_part = lax.dynamic_slice_in_dim(query_b, head_first, per_group, 1)
            key_part = lax.dynamic_slice_in_dim(keys_all, head_first, per_group, 1)
            value_part = lax.dynamic_slice_in_dim(values_all, head_first, per_group, 1)
            grad_part = lax.dynamic_slice_in_dim(grad_mixed_b, head_first, per_group, 1)
            log_part = lax.dynamic_slice_in_dim(log_totals, head_first, per_group, 0)
            scores = (
                jnp.einsum("qhe,khe->hqk", query_part, key_part, preferred_element_type=jnp.float32)
                / score_scale
            )
            scores = jnp.where(allowed[None], scores, -jnp.inf)
            probs = jnp.exp(scores - log_part[:, :, None])
            d_probs = jnp.einsum(
                "qhe,khe->hqk", grad_part, value_part, preferred_element_type=jnp.float32
            )
            row_dot = jnp.sum(probs * d_probs, axis=2)
            d_scores = (probs * (d_probs - row_dot[:, :, None])).astype(jnp.bfloat16)
            query_grad = (
                jnp.einsum("hqk,khe->qhe", d_scores, key_part, preferred_element_type=jnp.float32)
                / score_scale
            )
            d_query = lax.dynamic_update_slice_in_dim(d_query, query_grad, head_first, 1)
            row_dots = lax.dynamic_update_slice_in_dim(row_dots, row_dot, head_first, 0)
            key_grad = (
                jnp.einsum("hqk,qhe->khe", d_scores, query_part, preferred_element_type=jnp.float32)
                / score_scale
            )
            value_grad = jnp.einsum(
                "hqk,qhe->khe",
                probs.astype(jnp.bfloat16),
                grad_part,
                preferred_element_type=jnp.float32,
            )
            d_keys_values = lax.dynamic_update_slice_in_dim(
                d_keys_values, key_grad.reshape(group_rows, per_group * HEAD), head_first * HEAD, 1
            )
            d_keys_values = lax.dynamic_update_slice_in_dim(
                d_keys_values,
                value_grad.reshape(group_rows, per_group * HEAD),
                width + head_first * HEAD,
                1,
            )
            return (d_query, d_keys_values, row_dots)

        return backward_heads

    start_query = jnp.zeros((tok_rows, HEADS, HEAD), jnp.float32)
    start_dots = jnp.zeros((HEADS, tok_rows), jnp.float32)
    start_keys_values = jnp.zeros((group_rows, 2 * width), jnp.float32)
    d_query, d_keys_values, row_dots = lax.fori_loop(
        0, head_steps, make_backward(), (start_query, start_keys_values, start_dots)
    )
    d_kv_mine = lax.psum_scatter(d_keys_values, "ctx", scatter_dimension=0, tiled=True)
    key_rot_grad = d_kv_mine[:, :width].reshape(tok_rows, HEADS, HEAD)
    d_qkv_b = jnp.concatenate(
        [
            unrotate(d_query, cosine, sine).reshape(tok_rows, width),
            unrotate(key_rot_grad, cosine, sine).reshape(tok_rows, width),
            d_kv_mine[:, width:],
        ],
        axis=1,
    ).astype(jnp.bfloat16)
    qkv_part = dot_left_t(act_one, d_qkv_b)
    out_part = dot_left_t(attended_b, d_branch_b)
    attn_share = lax.psum_scatter(
        jnp.concatenate([qkv_part, out_part], axis=1).astype(jnp.bfloat16),
        "wa",
        scatter_dimension=0,
        tiled=True,
    )
    d_normed_one = dot_right_t(d_qkv_b, back_qkv)
    gain_one_part = jnp.sum(d_normed_one * normed_one, axis=0)
    scaled_one = d_normed_one * norm1_gain
    d_inputs = d_hidden + scale_one * (
        scaled_one - normed_one * jnp.mean(scaled_one * normed_one, axis=1, keepdims=True)
    )
    gain_one_sum, gain_two_sum = lax.psum((gain_one_part, gain_two_part), ("ctx", "wa"))
    attn_total, gate_up_total, down_total = (
        lax.psum(attn_share, "ctx").astype(jnp.float32),
        lax.psum(gate_up_share, "ctx").astype(jnp.float32),
        lax.psum(down_share, "ctx").astype(jnp.float32),
    )
    return (
        out_given[None],
        d_inputs.astype(jnp.bfloat16)[None],
        gain_one_sum,
        attn_total[:, : 3 * width],
        attn_total[:, 3 * width :],
        gain_two_sum,
        gate_up_total,
        down_total,
    )


def solution(mesh):
    in_specs = (
        P("wa", "ctx", None),
        P("wa", None),
        P("wa", None),
        P(),
        P("wa", None),
        P("wa", None),
        P(),
        P("wa", None),
        P("wa", None),
        P("wa", "ctx", None),
    )
    out_specs = (
        P("wa", "ctx", None),
        P("wa", "ctx", None),
        P(),
        P("wa", None),
        P("wa", None),
        P(),
        P("wa", None),
        P("wa", None),
    )
    return jax.shard_map(
        per_device, mesh=mesh, in_specs=in_specs, out_specs=out_specs, check_vma=False
    )
```

profile of v0, /device:TPU:0, one launch (start us, length us, event | category | flops | bytes accessed | tf_op | source)
XLA Modules:
  0.0 4124.8 jit_solution(4794331274431847272)
XLA Ops:
  9.7 427.8 %all-gather.9.cloned.1.call-done = bf16[2048,6144]{1,0:T(8,128)(2,1)} async-done(((bf16[512,6144]{1,0:T(8,128)(2,1)}), bf16[2048,6144]{1,0:T(8,128)(2,1)}) %all-gather.9.cloned.1.call-update) | async-done | bytes 25165840 | tf_op jit(solution)/shard_map/all_gather | solution.py:102
  437.5 10.5 fusion.58
  454.2 20.2 all-gather.21.cloned.1.call-done
  474.4 4.2 gather_fusion.1
  478.9 52.4 %all-gather.11.cloned.1.call-done = bf16[1024,4096]{1,0:T(8,128)(2,1)} async-done(((bf16[128,4096]{1,0:T(8,128)(2,1)}), bf16[1024,4096]{1,0:T(8,128)(2,1)}) %all-gather.11.cloned.1.call-update) | async-done | bytes 8388624 | tf_op jit(solution)/shard_map/all_gather | solution.py:114
  531.3 4.0 slice_bitcast_fusion.1
  546.7 135.7 %all-gather.13.cloned.1.call-done = bf16[2048,2048]{1,0:T(8,128)(2,1)} async-done(((bf16[512,2048]{1,0:T(8,128)(2,1)}), bf16[2048,2048]{1,0:T(8,128)(2,1)}) %all-gather.13.cloned.1.call-update) | async-done | bytes 8388624 | tf_op jit(solution)/shard_map/all_gather | solution.py:103
  682.4 4.8 multiply_reduce_fusion.3
  687.1 745.7 %all-gather.15.cloned.1.call-done = bf16[2048,11008]{1,0:T(8,128)(2,1)} async-done(((bf16[512,11008]{1,0:T(8,128)(2,1)}), bf16[2048,11008]{1,0:T(8,128)(2,1)}) %all-gather.15.cloned.1.call-update) | async-done | bytes 45088784 | tf_op jit(solution)/shard_map/all_gather | solution.py:144
  1432.8 24.1 fusion.64
  1456.9 358.1 %all-gather.17.cloned.1.call-done = bf16[5504,2048]{1,0:T(8,128)(2,1)} async-done(((bf16[1376,2048]{1,0:T(8,128)(2,1)}), bf16[5504,2048]{1,0:T(8,128)(2,1)}) %all-gather.17.cloned.1.call-update) | async-done | bytes 22544400 | tf_op jit(solution)/shard_map/all_gather | solution.py:145
  1815.0 14.9 multiply_convert_fusion.2
  1829.9 21.4 multiply_reduce_fusion.1
  1851.8 6.7 fusion.25
  1859.7 7.9 broadcast_in_dim.154
  1867.6 75.1 %while.18 = (s32[]{:T(128)}, f32[128,16,128]{2,0,1:T(8,128)}, f32[1024,4096]{0,1:T(8,128)}, bf16[1024,16,128]{2,0,1:T(8,128)(2,1)}, bf16[128,16,128]{2,0,1:T(8,1...) while((s32[]{:T(128)}, f32[128,16,128]{2,0,1:T(8,128)}, ...), condition=%wide.region_14.16_spmd.clone, body=%wide.region_12.15_spmd.clone.sunk | while | flops 677182976 | bytes 61174424 | solution.py:239
  1875.5 2.7 convolution_multiply_fusion.3
  1878.2 3.1 constant_dynamic-update-slice_fusion.7
  1883.2 3.3 constant_dynamic-update-slice_fusion.8
  1894.3 2.7 convolution_multiply_fusion.3
  1897.0 3.2 constant_dynamic-update-slice_fusion.7
  1902.0 3.2 constant_dynamic-update-slice_fusion.8
  1913.0 2.7 convolution_multiply_fusion.3
  1915.7 3.2 constant_dynamic-update-slice_fusion.7
  1920.7 3.2 constant_dynamic-update-slice_fusion.8
  1931.8 2.7 convolution_multiply_fusion.3
  1934.5 3.2 constant_dynamic-update-slice_fusion.7
  1939.5 3.2 constant_dynamic-update-slice_fusion.8
  1944.2 14.5 convolution_convert_fusion.1
  1960.8 20.6 convolution_convert_fusion
  1982.8 5.7 convolution_convert_fusion.3
  1988.5 68.8 %reduce-scatter.7.cloned.1.call-done = f32[128,4096]{0,1:T(8,128)} async-done(((f32[1024,4096]{0,1:T(8,128)}), f32[128,4096]{0,1:T(8,128)}) %reduce-scatter.7.cloned.1.call-update) | async-done | bytes 2097168 | tf_op jit(solution)/shard_map/reduce_scatter | solution.py:242
  2064.3 3.0 add_convert_fusion.1
  2076.1 13.2 convolution_convert_fusion.2
  2089.2 22.7 pad_maximum_fusion
  2112.0 11.9 fusion.19
  2124.2 308.3 %reduce-scatter.11.cloned.1.call-done = bf16[1376,2048]{1,0:T(8,128)(2,1)} async-done(((bf16[5504,2048]{1,0:T(8,128)(2,1)}), bf16[1376,2048]{1,0:T(8,128)(2,1)}) %reduce-scatter.11.cloned.1.call-update) | async-done | bytes 5636112 | tf_op jit(solution)/shard_map/reduce_scatter | solution.py:161
  2432.5 740.8 %reduce-scatter.9.cloned.1.call-done = bf16[512,11008]{1,0:T(8,128)(2,1)} async-done(((bf16[2048,11008]{1,0:T(8,128)(2,1)}), bf16[512,11008]{1,0:T(8,128)(2,1)}) %reduce-scatter.9.cloned.1.call-update) | async-done | bytes 11272208 | tf_op jit(solution)/shard_map/reduce_scatter | solution.py:167
  3173.3 556.0 %reduce-scatter.13.cloned.1.call-done = bf16[512,8192]{1,0:T(8,128)(2,1)} async-done(((bf16[2048,8192]{1,0:T(8,128)(2,1)}), bf16[512,8192]{1,0:T(8,128)(2,1)}) %reduce-scatter.13.cloned.1.call-update) | async-done | bytes 8388624
  3731.4 38.0 all-gather.19.cloned.1.call-done
  3769.4 5.0 gather_fusion
  3776.3 21.7 fusion.36
  3798.0 40.6 all-reduce.1
  3841.0 245.4 %all-reduce.5.cloned.1.call-done = (bf16[512,8192]{1,0:T(8,128)(2,1)}, bf16[512,11008]{1,0:T(8,128)(2,1)}, bf16[1376,2048]{1,0:T(8,128)(2,1)}) async-done(((bf16[512,8192]{1,0:T(8,128)(2,1)}, bf16[512,11008]{1,0:T(8,128)(2,1)}, bf16[1376,2048]{1,0:T(8,128)(2,1)}), (bf16[512,8192]{1,0:T(8,128)(2,1)}, bf16[512,11008]{1,0:T(8,128)(2,1)}, bf16[1376,2048]{1,0:T(8,128)(2,1)})) %all-reduce.5.cloned.1.call-update) | async-done | bytes 25296912 | tf_op jit(solution)/shard_map/psum | solution.py:268
  4086.3 9.4 slice.157
  4095.7 2.5 slice.158
  4098.3 13.3 convert_element_type.121
  4111.6 5.9 convert_element_type.123
  (300 shorter events, 86.0 us)
Async XLA Ops:
  7.2 430.3 %copy-start.28 = (f32[2048]{0:T(1024)S(1)}, f32[2048]{0:T(1024)}, u32[]{:S(2)}) copy-start(f32[2048]{0:T(1024)} %param.17) | copy-start | bytes 24580
  7.2 430.3 %all-gather.9.cloned.1.call-start = ((), (), s32[]{:S(2)}) async-start(), calls=%async_computation.4 | async-start | bytes 31457280 | tf_op jit(solution)/shard_map/all_gather | solution.py:102
  7.9 466.4 %all-gather.21.cloned.1.call-start = ((), (), s32[]{:S(2)}) async-start(), calls=%async_computation.13 | async-start | bytes 4718592 | tf_op jit(solution)/shard_map/all_gather | solution.py:95
  8.7 522.6 %all-gather.11.cloned.1.call-start = ((), (), s32[]{:S(2)}) async-start(), calls=%async_computation.5 | async-start | bytes 9437184 | tf_op jit(solution)/shard_map/all_gather | solution.py:114
  8.9 1842.4 %copy-start.41 = (pred[128]{0:T(512)(128)(4,1)}, pred[128]{0:T(512)(128)(4,1)S(1)}, u32[]{:S(2)}) copy-start(pred[128]{0:T(512)(128)(4,1)S(1)} %get-tuple-element.344) | copy-start | bytes 388
  9.1 438.9 %copy-start.37 = (f32[128]{0:T(128)}, f32[128]{0:T(128)S(1)}, u32[]{:S(2)}) copy-start(f32[128]{0:T(128)S(1)} %add_rsqrt_fusion.1) | copy-start | bytes 1540
  9.7 439.6 %copy-start.24 = (f32[128,64]{1,0:T(8,128)}, f32[128,64]{1,0:T(8,128)S(1)}, u32[]{:S(2)}) copy-start(f32[128,64]{1,0:T(8,128)S(1)} %get-tuple-element.381) | copy-start | bytes 98308
  9.7 439.6 %copy-start.26 = (f32[128,64]{1,0:T(8,128)}, f32[128,64]{1,0:T(8,128)S(1)}, u32[]{:S(2)}) copy-start(f32[128,64]{1,0:T(8,128)S(1)} %get-tuple-element.382) | copy-start | bytes 98308
  452.1 230.3 %all-gather.13.cloned.1.call-start = ((), (), s32[]{:S(2)}) async-start(), calls=%async_computation.6 | async-start | bytes 10485760 | tf_op jit(solution)/shard_map/all_gather | solution.py:103
  452.6 980.2 %all-gather.15.cloned.1.call-start = ((), (), s32[]{:S(2)}) async-start(), calls=%async_computation.7 | async-start | bytes 56360960 | tf_op jit(solution)/shard_map/all_gather | solution.py:144
  453.2 1361.8 %all-gather.17.cloned.1.call-start = ((), (), s32[]{:S(2)}) async-start(), calls=%async_computation.8 | async-start | bytes 28180480 | tf_op jit(solution)/shard_map/all_gather | solution.py:145
  453.8 1603.5 %reduce-scatter.7.cloned.1.call-start = ((), (), s32[]{:S(2)}) async-start(), calls=%async_computation.10 | async-start | bytes 18874368 | tf_op jit(solution)/shard_map/reduce_scatter | solution.py:242
  453.9 1397.5 %copy-start.44 = (pred[128]{0:T(512)(128)(4,1)}, pred[128]{0:T(512)(128)(4,1)S(1)}, u32[]{:S(2)}) copy-start(pred[128]{0:T(512)(128)(4,1)S(1)} %get-tuple-element.346) | copy-start | bytes 388
  478.5 1372.8 %copy-start.17 = (bf16[128,2048]{1,0:T(8,128)(2,1)}, bf16[128,2048]{1,0:T(8,128)(2,1)S(1)}, u32[]{:S(2)}) copy-start(bf16[128,2048]{1,0:T(8,128)(2,1)S(1)} %gather_fusion.1) | copy-start | bytes 1572868
  536.3 4.9 copy-start
  537.8 4.7 copy-start.2
  546.6 140.5 %copy-start.10 = (bf16[128,16,128]{0,2,1:T(8,128)(2,1)}, bf16[128,16,128]{0,2,1:T(8,128)(2,1)S(1)}, u32[]{:S(2)}) copy-start(bf16[128,16,128]{0,2,1:T(8,128)(2,1)S(1)} %pad_maximum_fusion.9) | copy-start | bytes 1572868
  682.4 750.5 %copy-start.23 = (f32[2048]{0:T(1024)S(1)}, f32[2048]{0:T(1024)}, u32[]{:S(2)}) copy-start(f32[2048]{0:T(1024)} %param.20) | copy-start | bytes 24580
  687.1 1164.2 %copy-start.3 = (f32[128,2048]{1,0:T(8,128)}, f32[128,2048]{1,0:T(8,128)S(1)}, u32[]{:S(2)}) copy-start(f32[128,2048]{1,0:T(8,128)S(1)} %get-tuple-element.392) | copy-start | bytes 3145732
  687.1 1164.2 %copy-start.30 = (f32[128]{0:T(128)}, f32[128]{0:T(128)S(1)}, u32[]{:S(2)}) copy-start(f32[128]{0:T(128)S(1)} %add_rsqrt_fusion) | copy-start | bytes 1540
  1851.8 6.7 copy-start.6
  1867.8 3.4 copy-start.14
  1867.8 3.4 copy-start.1
  1883.1 3.3 copy-start.35
  1883.1 3.3 copy-start.40
  1886.5 3.4 copy-start.14
  1886.6 3.4 copy-start.1
  1905.3 3.4 copy-start.14
  1905.3 3.4 copy-start.1
  1924.0 3.4 copy-start.14
  1924.1 3.4 copy-start.1
  1942.8 489.7 %reduce-scatter.11.cloned.1.call-start = ((), (), s32[]{:S(2)}) async-start(), calls=%async_computation.12 | async-start | bytes 28180480 | tf_op jit(solution)/shard_map/reduce_scatter | solution.py:161
  1958.7 1214.6 %reduce-scatter.9.cloned.1.call-start = ((), (), s32[]{:S(2)}) async-start(), calls=%async_computation.11 | async-start | bytes 56360960 | tf_op jit(solution)/shard_map/reduce_scatter | solution.py:167
  1981.4 1747.9 %reduce-scatter.13.cloned.1.call-start = ((), (), s32[]{:S(2)}) async-start(), calls=%async_computation.14 | async-start | bytes 41943040
  2057.3 7.0 copy-start.12
  2057.3 7.0 copy-start.25
  2057.3 7.0 copy-start.27
  2067.3 8.8 copy-start.9
  2067.3 8.8 copy-start.29
  2067.3 8.8 copy-start.38
  2111.9 1657.4 %all-gather.19.cloned.1.call-start = ((), (), s32[]{:S(2)}) async-start(), calls=%async_computation.9 | async-start | bytes 4718592 | tf_op jit(solution)/shard_map/all_gather | solution.py:155
  2123.9 1962.5 %all-reduce.5.cloned.1.call-start = ((), (), s32[]{:S(2)}) async-start(), calls=%async_computation.15 | async-start | bytes 50593792 | tf_op jit(solution)/shard_map/psum | solution.py:268
  3731.3 45.0 %copy-start.21 = (bf16[128,16,128]{0,2,1:T(8,128)(2,1)S(1)}, bf16[128,16,128]{0,2,1:T(8,128)(2,1)}, u32[]{:S(2)}) copy-start(bf16[128,16,128]{0,2,1:T(8,128)(2,1)} %copy.113) | copy-start | bytes 1572868
  3731.4 45.0 %copy-start.22 = (bf16[128,2048]{0,1:T(8,128)(2,1)S(1)}, bf16[128,2048]{0,1:T(8,128)(2,1)}, u32[]{:S(2)}) copy-start(bf16[128,2048]{0,1:T(8,128)(2,1)} %slice.185) | copy-start | bytes 1572868
  3776.3 21.7 copy-start.36
  4086.3 9.4 copy-start.5
  4095.7 15.8 slice-start
  4098.2 13.3 slice-start.1
  (48 other events, 129.9 us)
Sparse Core Ops, SparseCore 0:
  9.6 427.8 all-gather.8
  439.4 34.8 all-gather.20
  476.8 54.3 all-gather.10
  532.7 149.6 all-gather.12
  683.8 748.9 all-gather.14
  1434.2 380.7 all-gather.16
  1942.9 114.3 reduce-scatter.6
  2060.2 372.2 reduce-scatter.10
  2434.9 738.3 reduce-scatter.8
  3175.5 553.7 reduce-scatter.12
  3731.9 37.4 all-gather.18
  3774.0 312.2 all-reduce.4
where the time goes:
time: 4130 us; the launch traced here: 4120 us
  waiting for transfers between devices  3700 us (90%)
  matrix products  201 us (5%)
  local copies, waits for them, and re-layouts  104 us (3%)
  other arithmetic  61.5 us (1%)
    all_gather x1, waiting for transfers between devices, per_device(): lax.all_gather(w_gate_up, 'wa', axis=0, tiled=True)  746 us
    reduce_scatter x1, waiting for transfers between devices, per_device(): lax.psum_scatter(dot_left_t(act_two, d_gate_up_b).astype(jnp.bfloat16), '...  741 us
    unnamed x13, waiting for transfers between devices  559 us
    all_gather x1, waiting for transfers between devices, per_device(): lax.all_gather(w_qkv, 'wa', axis=0, tiled=True)  428 us
    all_gather x1, waiting for transfers between devices, per_device(): lax.all_gather(w_down, 'wa', axis=0, tiled=True)  358 us
    reduce_scatter x1, waiting for transfers between devices, per_device(): lax.psum_scatter(dot_left_t(inner_b, cotangent).astype(jnp.bfloat16), 'wa...  308 us
    psum x1, waiting for transfers between devices, per_device(): lax.psum(attn_share, 'ctx').astype(jnp.float32)  245 us
    all_gather x1, waiting for transfers between devices, per_device(): lax.all_gather(w_out, 'wa', axis=0, tiled=True)  136 us
  transfers between devices with their start and end apart: 12, of which 12 were waited for; matrix products, arithmetic and copies ran while one was open for 5% of the time, Pallas kernels for 0%

commit v1 on v0

--- a/solution.py
+++ b/solution.py
@@ -1,8 +1,10 @@
+import functools
 import math
 import jax
 import jax.numpy as jnp
 from jax import lax
 from jax.sharding import PartitionSpec as P
+from jax.lax import axis_index, axis_size, ppermute
 
 HEADS = 16
 HEAD = 128
@@ -10,6 +12,25 @@
 WINDOW = 2048
 BLOCK = 128
 EPSILON = 1e-06
+
+
+def knots_lay(tile_in, named_axis):
+    world = axis_size(named_axis)
+    line_up = [tile_in]
+    for t in range(1, world):
+        line_up.append(
+            ppermute(
+                line_up[t - 1],
+                axis_name=named_axis,
+                perm=[(j0, (j0 - 1) % world) for j0 in range(world)],
+            )
+        )
+    prior = jnp.concatenate(line_up, 0)
+    a_now = jnp.roll(prior, axis_index(named_axis) * tile_in.shape[0], 0)
+    return a_now
+
+
+solve_run = functools.partial(knots_lay, named_axis="wa")
 
 
 def dot_plain(left, right):
@@ -98,10 +119,7 @@
     scale_one = rms_scale(inputs)
     normed_one = inputs * scale_one
     act_one = (normed_one * norm1_gain).astype(jnp.bfloat16)
-    full_qkv, full_out = (
-        lax.all_gather(w_qkv, "wa", axis=0, tiled=True),
-        lax.all_gather(w_out, "wa", axis=0, tiled=True),
-    )
+    full_qkv, full_out = (solve_run(w_qkv), lax.all_gather(w_out, "wa", axis=0, tiled=True))
     projected = dot_plain(act_one, full_qkv)
     query_b = rotate(projected[:, :width].reshape(tok_rows, HEADS, HEAD), cosine, sine).astype(
         jnp.bfloat16

time: 4130 us -> 4560 us (1.10)
  waiting for transfers between devices: 3700 us -> 4060 us
  local copies, waits for them, and re-layouts: 104 us -> 150 us
    ppermute x0 -> x3, waiting for transfers between devices: none -> 382 us  [knots_lay(): ppermute(line_up[t - 1], axis_name=named_axis, perm=[(j0, (j0 - 1) % worl...]
  transfers between devices with their start and end apart: 12 -> 15, of which waited for: 12 -> 14; matrix products, arithmetic and copies ran while one was open for 5% -> 6% of each run, Pallas kernels for 0% -> 0%
where the time goes in v1:
time: 4560 us; the launch traced here: 4550 us
  waiting for transfers between devices  4060 us (89%)
  matrix products  203 us (4%)
  local copies, waits for them, and re-layouts  150 us (3%)
  other arithmetic  64.9 us (1%)
    all_gather x1, waiting for transfers between devices, per_device(): lax.all_gather(w_gate_up, 'wa', axis=0, tiled=True)  746 us
    reduce_scatter x1, waiting for transfers between devices, per_device(): lax.psum_scatter(dot_left_t(act_two, d_gate_up_b).astype(jnp.bfloat16), '...  741 us
    unnamed x13, waiting for transfers between devices  558 us
    all_gather x1, waiting for transfers between devices, per_device(): lax.all_gather(w_qkv, 'wa', axis=0, tiled=True)  420 us
    ppermute x3, waiting for transfers between devices, knots_lay(): ppermute(line_up[t - 1], axis_name=named_axis, perm=[(j0, (j0 - 1) % worl...  382 us
    all_gather x1, waiting for transfers between devices, per_device(): lax.all_gather(w_down, 'wa', axis=0, tiled=True)  358 us
    reduce_scatter x1, waiting for transfers between devices, per_device(): lax.psum_scatter(dot_left_t(inner_b, cotangent).astype(jnp.bfloat16), 'wa...  307 us
    psum x1, waiting for transfers between devices, per_device(): lax.psum(attn_share, 'ctx').astype(jnp.float32)  252 us
  transfers between devices with their start and end apart: 15, of which 14 were waited for; matrix products, arithmetic and copies ran while one was open for 6% of the time, Pallas kernels for 0%

profile of v1, /device:TPU:0, one launch (start us, length us, event | category | flops | bytes accessed | tf_op | source)
XLA Modules:
  0.0 4546.0 jit_solution(18290365159471502219)
XLA Ops:
  7.2 5.1 collective-permute-start
  12.3 135.1 %collective-permute-done = bf16[512,6144]{1,0:T(8,128)(2,1)S(1)} collective-permute-done((bf16[512,6144]{1,0:T(8,128)(2,1)}, bf16[512,6144]{1,0:T(8,128)(2,1)S(1)}, u32[]{:S(2)}, u32[]{:S(2)}) %collective-permute-start) | collective-permute-done | bytes 6291488 | tf_op jit(solution)/shard_map/ppermute | solution.py:22
  150.1 4.2 collective-permute-start.1
  154.3 133.9 %collective-permute-done.1 = bf16[512,6144]{1,0:T(8,128)(2,1)} collective-permute-done((bf16[512,6144]{1,0:T(8,128)(2,1)S(1)}, bf16[512,6144]{1,0:T(8,128)(2,1)}, u32[]{:S(2)}, u32[]{:S(2)}) %collective-permute-start.1) | collective-permute-done | bytes 6291488 | tf_op jit(solution)/shard_map/ppermute | solution.py:22
  288.2 4.4 collective-permute-start.2
  296.5 6.9 constant_dynamic-update-slice_fusion.10
  306.5 6.3 constant_dynamic-update-slice_fusion.8
  312.8 113.1 %collective-permute-done.2 = bf16[512,6144]{1,0:T(8,128)(2,1)} collective-permute-done((bf16[512,6144]{1,0:T(8,128)(2,1)}, bf16[512,6144]{1,0:T(8,128)(2,1)}, u32[]{:S(2)}, u32[]{:S(2)}) %collective-permute-start.2) | collective-permute-done | bytes 6291488 | tf_op jit(solution)/shard_map/ppermute | solution.py:22
  425.9 6.2 constant_dynamic-update-slice_fusion.7
  438.3 6.1 constant_dynamic-update-slice_fusion.4
  444.5 6.2 constant_dynamic-update-slice_fusion.3
  450.7 13.4 fusion.18
  473.4 4.2 gather_fusion.1
  477.9 49.5 %all-gather.9.cloned.1.call-done = bf16[1024,4096]{1,0:T(8,128)(2,1)} async-done(((bf16[128,4096]{1,0:T(8,128)(2,1)}), bf16[1024,4096]{1,0:T(8,128)(2,1)}) %all-gather.9.cloned.1.call-update) | async-done | bytes 8388624 | tf_op jit(solution)/shard_map/all_gather | solution.py:132
  527.4 3.8 slice_bitcast_fusion.1
  542.6 136.0 %all-gather.11.cloned.1.call-done = bf16[2048,2048]{1,0:T(8,128)(2,1)} async-done(((bf16[512,2048]{1,0:T(8,128)(2,1)}), bf16[2048,2048]{1,0:T(8,128)(2,1)}) %all-gather.11.cloned.1.call-update) | async-done | bytes 8388624 | tf_op jit(solution)/shard_map/all_gather | solution.py:122
  678.6 4.8 multiply_reduce_fusion.3
  683.4 745.7 %all-gather.13.cloned.1.call-done = bf16[2048,11008]{1,0:T(8,128)(2,1)} async-done(((bf16[512,11008]{1,0:T(8,128)(2,1)}), bf16[2048,11008]{1,0:T(8,128)(2,1)}) %all-gather.13.cloned.1.call-update) | async-done | bytes 45088784 | tf_op jit(solution)/shard_map/all_gather | solution.py:162
  1429.1 24.1 fusion.66
  1453.2 358.1 %all-gather.15.cloned.1.call-done = bf16[5504,2048]{1,0:T(8,128)(2,1)} async-done(((bf16[1376,2048]{1,0:T(8,128)(2,1)}), bf16[5504,2048]{1,0:T(8,128)(2,1)}) %all-gather.15.cloned.1.call-update) | async-done | bytes 22544400 | tf_op jit(solution)/shard_map/all_gather | solution.py:163
  1811.3 14.9 multiply_convert_fusion.2
  1826.1 21.4 multiply_reduce_fusion.1
  1848.0 6.7 fusion.27
  1855.8 7.9 broadcast_in_dim.154
  1863.7 75.1 %while.18 = (s32[]{:T(128)}, f32[128,16,128]{2,0,1:T(8,128)}, f32[1024,4096]{0,1:T(8,128)}, bf16[1024,16,128]{2,0,1:T(8,128)(2,1)}, bf16[128,16,128]{2,0,1:T(8,1...) while((s32[]{:T(128)}, f32[128,16,128]{2,0,1:T(8,128)}, ...), condition=%wide.region_14.16_spmd.clone, body=%wide.region_12.15_spmd.clone.sunk | while | flops 677182976 | bytes 61174424 | solution.py:257
  1879.3 3.2 constant_dynamic-update-slice_fusion.16
  1898.0 3.2 constant_dynamic-update-slice_fusion.16
  1916.7 3.3 constant_dynamic-update-slice_fusion.16
  1935.5 3.2 constant_dynamic-update-slice_fusion.16
  1940.3 14.5 convolution_convert_fusion.1
  1956.8 20.6 convolution_convert_fusion
  1978.8 5.7 convolution_convert_fusion.3
  1984.6 68.8 %reduce-scatter.7.cloned.1.call-done = f32[128,4096]{0,1:T(8,128)} async-done(((f32[1024,4096]{0,1:T(8,128)}), f32[128,4096]{0,1:T(8,128)}) %reduce-scatter.7.cloned.1.call-update) | async-done | bytes 2097168 | tf_op jit(solution)/shard_map/reduce_scatter | solution.py:260
  2072.3 13.1 convolution_convert_fusion.2
  2085.4 23.2 pad_maximum_fusion
  2108.6 11.8 fusion.21
  2121.3 307.3 %reduce-scatter.11.cloned.1.call-done = bf16[1376,2048]{1,0:T(8,128)(2,1)} async-done(((bf16[5504,2048]{1,0:T(8,128)(2,1)}), bf16[1376,2048]{1,0:T(8,128)(2,1)}) %reduce-scatter.11.cloned.1.call-update) | async-done | bytes 5636112 | tf_op jit(solution)/shard_map/reduce_scatter | solution.py:179
  2428.6 740.8 %reduce-scatter.9.cloned.1.call-done = bf16[512,11008]{1,0:T(8,128)(2,1)} async-done(((bf16[2048,11008]{1,0:T(8,128)(2,1)}), bf16[512,11008]{1,0:T(8,128)(2,1)}) %reduce-scatter.9.cloned.1.call-update) | async-done | bytes 11272208 | tf_op jit(solution)/shard_map/reduce_scatter | solution.py:185
  3169.4 556.1 %reduce-scatter.13.cloned.1.call-done = bf16[512,8192]{1,0:T(8,128)(2,1)} async-done(((bf16[2048,8192]{1,0:T(8,128)(2,1)}), bf16[512,8192]{1,0:T(8,128)(2,1)}) %reduce-scatter.13.cloned.1.call-update) | async-done | bytes 8388624
  3727.6 37.9 all-gather.17.cloned.1.call-done
  3765.5 5.0 gather_fusion
  3772.4 419.9 %all-gather.19.cloned.1.call-done = bf16[2048,6144]{1,0:T(8,128)(2,1)} async-done(((bf16[512,6144]{1,0:T(8,128)(2,1)}), bf16[2048,6144]{1,0:T(8,128)(2,1)}) %all-gather.19.cloned.1.call-update) | async-done | bytes 25165840 | tf_op jit(solution)/shard_map/all_gather | solution.py:196
  4192.3 20.5 fusion.38
  4212.9 40.3 all-reduce.1
  4255.5 252.0 %all-reduce.5.cloned.1.call-done = (bf16[512,8192]{1,0:T(8,128)(2,1)}, bf16[512,11008]{1,0:T(8,128)(2,1)}, bf16[1376,2048]{1,0:T(8,128)(2,1)}) async-done(((bf16[512,8192]{1,0:T(8,128)(2,1)}, bf16[512,11008]{1,0:T(8,128)(2,1)}, bf16[1376,2048]{1,0:T(8,128)(2,1)}), (bf16[512,8192]{1,0:T(8,128)(2,1)}, bf16[512,11008]{1,0:T(8,128)(2,1)}, bf16[1376,2048]{1,0:T(8,128)(2,1)})) %all-reduce.5.cloned.1.call-update) | async-done | bytes 25296912 | tf_op jit(solution)/shard_map/psum | solution.py:286
  4507.5 9.4 slice.157
  4519.4 13.3 convert_element_type.121
  4532.7 5.9 convert_element_type.123
  (321 shorter events, 132.2 us)
Async XLA Ops:
  7.2 466.2 %all-gather.21.cloned.1.call-start = ((), (), s32[]{:S(2)}) async-start(), calls=%async_computation.13 | async-start | bytes 4718592 | tf_op jit(solution)/shard_map/all_gather | solution.py:116
  7.2 140.2 %collective-permute-start = (bf16[512,6144]{1,0:T(8,128)(2,1)}, bf16[512,6144]{1,0:T(8,128)(2,1)S(1)}, u32[]{:S(2)}, u32[]{:S(2)}) collective-permute-start(bf16[512,6144]{1,0:T(8,128)(2,1)} %param.18), channel_id=1, source_target_pairs={{0,3},{1,0},{2,1},{3,2},{4,7},{5,4},{6,5},{7,6},{8,11},{9,8},{10,9... | collective-permute-start | bytes 18874376 | tf_op jit(solution)/shard_map/ppermute | solution.py:22
  150.1 138.1 %collective-permute-start.1 = (bf16[512,6144]{1,0:T(8,128)(2,1)S(1)}, bf16[512,6144]{1,0:T(8,128)(2,1)}, u32[]{:S(2)}, u32[]{:S(2)}) collective-permute-start(bf16[512,6144]{1,0:T(8,128)(2,1)S(1)} %collective-permute-done), channel_id=1, source_target_pairs={{0,3},{1,0},{2,1},{3,2},{4,7},{5,4},{6,5},{7,6},{8,11},{9,8},{10,9... | collective-permute-start | bytes 18874376 | tf_op jit(solution)/shard_map/ppermute | solution.py:22
  288.2 137.7 %collective-permute-start.2 = (bf16[512,6144]{1,0:T(8,128)(2,1)}, bf16[512,6144]{1,0:T(8,128)(2,1)}, u32[]{:S(2)}, u32[]{:S(2)}) collective-permute-start(bf16[512,6144]{1,0:T(8,128)(2,1)} %collective-permute-done.1), channel_id=1, source_target_pairs={{0,3},{1,0},{2,1},{3,2},{4,7},{5,4},{6,5},{7,6},{8,11},{9,8},{10,9... | collective-permute-start | bytes 18874376 | tf_op jit(solution)/shard_map/ppermute | solution.py:22
  292.6 234.8 %all-gather.9.cloned.1.call-start = ((), (), s32[]{:S(2)}) async-start(), calls=%async_computation.4 | async-start | bytes 9437184 | tf_op jit(solution)/shard_map/all_gather | solution.py:132
  293.5 1554.0 %copy-start.42 = (pred[128]{0:T(512)(128)(4,1)}, pred[128]{0:T(512)(128)(4,1)S(1)}, u32[]{:S(2)}) copy-start(pred[128]{0:T(512)(128)(4,1)S(1)} %get-tuple-element.344) | copy-start | bytes 388
  294.7 156.0 %copy-start.40 = (f32[128]{0:T(128)}, f32[128]{0:T(128)S(1)}, u32[]{:S(2)}) copy-start(f32[128]{0:T(128)S(1)} %add_rsqrt_fusion.1) | copy-start | bytes 1540
  296.2 7.2 slice-start.2
  296.5 171.7 %copy-start.25 = (f32[128,64]{1,0:T(8,128)}, f32[128,64]{1,0:T(8,128)S(1)}, u32[]{:S(2)}) copy-start(f32[128,64]{1,0:T(8,128)S(1)} %get-tuple-element.381) | copy-start | bytes 98308
  296.5 171.7 %copy-start.27 = (f32[128,64]{1,0:T(8,128)}, f32[128,64]{1,0:T(8,128)S(1)}, u32[]{:S(2)}) copy-start(f32[128,64]{1,0:T(8,128)S(1)} %get-tuple-element.382) | copy-start | bytes 98308
  296.5 6.9 slice-start.3
  306.5 125.6 %slice-start = ((s8[6291456]{0:T(1024)(128)(4,1)}), s8[4194304]{0:T(1024)(128)(4,1)S(1)}, s32[]{:S(2)}) async-start(s8[6291456]{0:T(1024)(128)(4,1)} %bitcast.96), calls=%async_computation.16 | async-start | bytes 8388608
  312.8 119.3 %slice-start.1 = ((s8[6291456]{0:T(1024)(128)(4,1)}), s8[2097152]{0:T(1024)(128)(4,1)S(1)}, s32[]{:S(2)}) async-start(s8[6291456]{0:T(1024)(128)(4,1)} %bitcast.96), calls=%async_computation.17 | async-start | bytes 4194304
  444.5 6.2 copy-start.11
  444.5 6.3 copy-start.29
  470.9 207.7 %all-gather.11.cloned.1.call-start = ((), (), s32[]{:S(2)}) async-start(), calls=%async_computation.5 | async-start | bytes 10485760 | tf_op jit(solution)/shard_map/all_gather | solution.py:122
  471.6 957.4 %all-gather.13.cloned.1.call-start = ((), (), s32[]{:S(2)}) async-start(), calls=%async_computation.6 | async-start | bytes 56360960 | tf_op jit(solution)/shard_map/all_gather | solution.py:162
  472.2 1339.0 %all-gather.15.cloned.1.call-start = ((), (), s32[]{:S(2)}) async-start(), calls=%async_computation.7 | async-start | bytes 28180480 | tf_op jit(solution)/shard_map/all_gather | solution.py:163
  472.8 1580.6 %reduce-scatter.7.cloned.1.call-start = ((), (), s32[]{:S(2)}) async-start(), calls=%async_computation.9 | async-start | bytes 18874368 | tf_op jit(solution)/shard_map/reduce_scatter | solution.py:260
  473.1 1374.5 %copy-start.44 = (pred[128]{0:T(512)(128)(4,1)}, pred[128]{0:T(512)(128)(4,1)S(1)}, u32[]{:S(2)}) copy-start(pred[128]{0:T(512)(128)(4,1)S(1)} %get-tuple-element.346) | copy-start | bytes 388
  477.6 1370.0 %copy-start.18 = (bf16[128,2048]{1,0:T(8,128)(2,1)}, bf16[128,2048]{1,0:T(8,128)(2,1)S(1)}, u32[]{:S(2)}) copy-start(bf16[128,2048]{1,0:T(8,128)(2,1)S(1)} %gather_fusion.1) | copy-start | bytes 1572868
  532.3 4.9 copy-start
  533.7 4.7 copy-start.2
  542.6 140.8 %copy-start.9 = (bf16[128,16,128]{0,2,1:T(8,128)(2,1)}, bf16[128,16,128]{0,2,1:T(8,128)(2,1)S(1)}, u32[]{:S(2)}) copy-start(bf16[128,16,128]{0,2,1:T(8,128)(2,1)S(1)} %pad_maximum_fusion.9) | copy-start | bytes 1572868
  678.6 750.5 %copy-start.24 = (f32[2048]{0:T(1024)S(1)}, f32[2048]{0:T(1024)}, u32[]{:S(2)}) copy-start(f32[2048]{0:T(1024)} %param.20) | copy-start | bytes 24580
  683.4 1164.2 %copy-start.3 = (f32[128,2048]{1,0:T(8,128)}, f32[128,2048]{1,0:T(8,128)S(1)}, u32[]{:S(2)}) copy-start(f32[128,2048]{1,0:T(8,128)S(1)} %get-tuple-element.392) | copy-start | bytes 3145732
  683.4 1164.2 %copy-start.31 = (f32[128]{0:T(128)}, f32[128]{0:T(128)S(1)}, u32[]{:S(2)}) copy-start(f32[128]{0:T(128)S(1)} %add_rsqrt_fusion) | copy-start | bytes 1540
  1848.0 6.7 copy-start.7
  1901.3 4.4 copy-start.15
  1920.1 4.4 copy-start.15
  1938.9 489.7 %reduce-scatter.11.cloned.1.call-start = ((), (), s32[]{:S(2)}) async-start(), calls=%async_computation.12 | async-start | bytes 28180480 | tf_op jit(solution)/shard_map/reduce_scatter | solution.py:179
  1954.8 1214.6 %reduce-scatter.9.cloned.1.call-start = ((), (), s32[]{:S(2)}) async-start(), calls=%async_computation.11 | async-start | bytes 56360960 | tf_op jit(solution)/shard_map/reduce_scatter | solution.py:185
  1977.5 1748.0 %reduce-scatter.13.cloned.1.call-start = ((), (), s32[]{:S(2)}) async-start(), calls=%async_computation.14 | async-start | bytes 41943040
  2054.7 5.8 copy-start.13
  2054.7 5.8 copy-start.26
  2054.7 5.8 copy-start.28
  2063.4 8.8 copy-start.12
  2063.4 8.8 copy-start.30
  2063.4 8.8 copy-start.41
  2108.6 1656.9 %all-gather.17.cloned.1.call-start = ((), (), s32[]{:S(2)}) async-start(), calls=%async_computation.8 | async-start | bytes 4718592 | tf_op jit(solution)/shard_map/all_gather | solution.py:173
  2120.5 2071.8 %all-gather.19.cloned.1.call-start = ((), (), s32[]{:S(2)}) async-start(), calls=%async_computation.10 | async-start | bytes 31457280 | tf_op jit(solution)/shard_map/all_gather | solution.py:196
  2121.2 2386.2 %all-reduce.5.cloned.1.call-start = ((), (), s32[]{:S(2)}) async-start(), calls=%async_computation.15 | async-start | bytes 50593792 | tf_op jit(solution)/shard_map/psum | solution.py:286
  3725.5 466.8 %copy-start.22 = (bf16[128,16,128]{0,2,1:T(8,128)(2,1)S(1)}, bf16[128,16,128]{0,2,1:T(8,128)(2,1)}, u32[]{:S(2)}) copy-start(bf16[128,16,128]{0,2,1:T(8,128)(2,1)} %copy.113) | copy-start | bytes 1572868
  3725.6 466.8 %copy-start.23 = (bf16[128,2048]{0,1:T(8,128)(2,1)S(1)}, bf16[128,2048]{0,1:T(8,128)(2,1)}, u32[]{:S(2)}) copy-start(bf16[128,2048]{0,1:T(8,128)(2,1)} %slice.185) | copy-start | bytes 1572868
  3772.4 440.5 %copy-start.37 = (f32[2048]{0:T(1024)S(1)}, f32[2048]{0:T(1024)}, u32[]{:S(2)}) copy-start(f32[2048]{0:T(1024)} %get-tuple-element.311) | copy-start | bytes 24580
  4507.5 9.4 copy-start.5
  4516.9 15.8 slice-start.4
  4519.4 13.3 slice-start.5
  (53 other events, 165.0 us)
Sparse Core Ops, SparseCore 0:
  292.7 34.9 all-gather.20
  471.0 56.3 all-gather.8
  528.9 149.6 all-gather.10
  680.1 748.9 all-gather.12
  1430.5 380.7 all-gather.14
  1939.0 114.3 reduce-scatter.6
  2056.3 372.2 reduce-scatter.10
  2431.0 738.3 reduce-scatter.8
  3171.7 553.7 reduce-scatter.12
  3728.0 37.4 all-gather.16
  3767.1 425.1 all-gather.18
  4197.0 310.4 all-reduce.4
